TPU v7x, 32 devices: a whole 2x2x4 slice. The times are simulated.
32 devices in a mesh: shot: 8 (over z, x), lag: 4 (over y, core).
Axes of the slice: x: 2, y: 2, z: 4, core: 2. Of those that a mesh axis runs over, the one named last changes fastest.
Arguments:
- traces: bfloat16 [48, 256, 8192], P('shot', 'lag'), may hold values from -64 to 64, as said below
- live_mask: int32 [48, 256], P('shot', 'lag'), may hold values 0 or 1
- gap_samples: int32 [1], replicated, may hold values from 1 to 32
Outputs:
- residual_traces: bfloat16 [48, 256, 8192], P('shot', 'lag')
Inputs may be any that keep to these rules, and one draw needn't show every extreme that they name: `traces`: recorded samples.
All inputs are finite; a program needn't handle non-finite values. No bound on the sum of `live_mask` on one device may be relied on, other than what follows from the above.
Results may differ from a plain program's by a relative error of at most 0.015.
The roundings to bfloat16 on the way count: a program that leaves them out, or rounds other values in their place, can miss the bound.
Values may be sent and summed in bfloat16 or wider, within the bound.
A program may use at most 128 MiB of HBM per device.

v0:
```python
import jax
import jax.numpy as jnp
from jax import lax
from jax.sharding import PartitionSpec as P

LAGS = 4


def dft_table(first_row, row_count, samples, band_size):
    times_idx = jnp.arange(row_count, dtype=jnp.int32) + first_row
    harmonic = jnp.arange(1, band_size + 1, dtype=jnp.int32)
    phase = times_idx[:, None] * harmonic[None, :] % (2 * samples)
    angle = phase.astype(jnp.float32) * (jnp.pi / samples)
    return jnp.concatenate([jnp.cos(angle), jnp.sin(angle)], axis=1).astype(jnp.bfloat16)


def delay_tables(delays, samples, band_size):
    harmonic = jnp.arange(1, band_size + 1, dtype=jnp.int32)
    phase = delays[:, None] * harmonic[None, :] % (2 * samples)
    angle = phase.astype(jnp.float32) * (jnp.pi / samples)
    return (jnp.cos(angle), jnp.sin(angle))


def delay_apply(spectrum, cosine, sine):
    band_size = cosine.shape[-1]
    real_part = spectrum[..., :band_size]
    imag_part = spectrum[..., band_size:]
    return jnp.concatenate(
        [real_part * cosine - imag_part * sine, imag_part * cosine + real_part * sine], axis=-1
    )


def shards(traces, live_mask, gap_samples):
    shot_count, local_chan, samples = traces.shape
    band_size = samples // 16
    block_len = min(1024, samples)
    live_bf = live_mask.astype(jnp.bfloat16)
    masked = traces * live_bf[:, :, None]
    running = jnp.zeros((shot_count, local_chan, 2 * band_size), jnp.float32)
    for offset in range(0, samples, block_len):
        table = dft_table(offset, block_len, samples, band_size)
        running = running + jnp.einsum(
            "sct,tw->scw",
            masked[:, :, offset : offset + block_len],
            table,
            preferred_element_type=jnp.float32,
        )
    own_spec = running.astype(jnp.bfloat16)
    all_spec = lax.all_gather(own_spec, "lag", axis=1, tiled=True)
    spacing = samples // (2 * band_size)
    tap_delays = jnp.arange(LAGS, dtype=jnp.int32) * spacing
    lag_list = jnp.concatenate([tap_delays, gap_samples[0] + tap_delays])
    cosine, sine = delay_tables(lag_list, samples, band_size)
    rotated = delay_apply(
        own_spec.astype(jnp.float32)[None], cosine[:, None, None, :], sine[:, None, None, :]
    ).astype(jnp.bfloat16)
    partial_value = jnp.einsum(
        "ksaf,sbf->kab", rotated, all_spec, preferred_element_type=jnp.float32
    )
    summed = lax.psum(partial_value, "shot")
    total_shots = shot_count * lax.axis_size("shot")
    gathered = lax.all_gather(summed, "lag", axis=1, tiled=True)
    correlation = gathered * (1.0 / samples) * (1.0 / (samples * total_shots))
    channels = correlation.shape[1]
    whiten = 0.1 * jnp.mean(jnp.diagonal(correlation[0])) + 1e-06
    zero_lag = correlation[0] + whiten * jnp.eye(channels, dtype=jnp.float32)
    weighted = jnp.concatenate([zero_lag[None], correlation[1:]], axis=0)
    lag_index = lax.axis_index("lag")
    first_out = lag_index * local_chan
    rhs = jnp.concatenate(
        [
            lax.dynamic_slice(weighted[LAGS + row_block], (0, first_out), (channels, local_chan))
            for row_block in range(LAGS)
        ],
        axis=0,
    )
    blocks = []
    for row_block in range(LAGS):
        row_parts = []
        for col_section in range(LAGS):
            if row_block >= col_section:
                row_parts.append(weighted[row_block - col_section])
            else:
                row_parts.append(weighted[col_section - row_block].T)
        blocks.append(jnp.concatenate(row_parts, axis=1))
    system = jnp.concatenate(blocks, axis=0)
    lower_factor = jnp.linalg.cholesky(system)
    filter_own = jax.scipy.linalg.cho_solve((lower_factor, True), rhs)
    filter_bf = filter_own.astype(jnp.bfloat16).reshape(LAGS, channels, local_chan)
    mixed = jnp.einsum("jab,saf->jsbf", filter_bf, all_spec, preferred_element_type=jnp.float32)
    shifted = delay_apply(mixed, cosine[LAGS:, None, None, :], sine[LAGS:, None, None, :])
    predicted = jnp.sum(shifted, axis=0)
    error = (own_spec.astype(jnp.float32) - predicted).astype(jnp.bfloat16)
    live_float = live_bf.astype(jnp.float32)[:, :, None]
    outputs = []
    for offset in range(0, samples, block_len):
        table = dft_table(offset, block_len, samples, band_size)
        restored = jnp.einsum("scw,tw->sct", error, table, preferred_element_type=jnp.float32)
        outputs.append((restored * (1.0 / samples) * live_float).astype(jnp.bfloat16))
    return jnp.concatenate(outputs, axis=2)


def solution(mesh):
    placed = (P("shot", "lag", None), P("shot", "lag"), P())
    return jax.shard_map(
        shards, mesh=mesh, in_specs=placed, out_specs=P("shot", "lag", None), check_vma=False
    )
```

profile of v0, /device:TPU:0, one launch (start us, length us, event | category | flops | bytes accessed | tf_op | source)
XLA Modules:
  0.0 613.0 jit_solution(16711117287114105271)
XLA Ops:
  7.3 3.3 broadcast_multiply_fusion
  10.5 68.2 %cosine_convert_fusion = (bf16[1024,512]{1,0:T(8,128)(2,1)S(1)}, bf16[1024,512]{1,0:T(8,128)(2,1)S(1)}, bf16[1024,512]{1,0:T(8,128)(2,1)S(1)}, bf16[1024,512]{1,...) fusion(s32[512]{0:T(512)S(1)} %iota_add_fusion.7, ...), kind=kLoop, calls=%fused_computation.93 | loop fusion | flops 67108864 | bytes 16807936 | tf_op jit(solution)/shard_map/convert.10
  91.2 4.5 subtract_convert_fusion
  95.7 24.5 %all-gather.3.cloned.1.call-done = bf16[6,256,1024]{2,1,0:T(8,128)(2,1)} async-done(((bf16[6,64,1024]{2,1,0:T(8,128)(2,1)}), bf16[6,256,1024]{2,1,0:T(8,128)(2,1)}) %all-gather.3.cloned.1.call-update) | async-done | bytes 3145744 | tf_op jit(solution)/shard_map/all_gather | solution.py:49
  120.2 6.4 %fusion.54 = f32[8,64,256]{2,1,0:T(8,128)} fusion(bf16[6,256,1024]{2,1,0:T(8,128)(2,1)} %all-gather.3.cloned.1.call-done, bf16[8,6,64,512]{3,2,1,0:T(8,128)(2,1)} %get-tuple-element.39, bf16[8,6,64,512]{3,2,1,0:T(8,128)(2,1)} %get-tuple-element.38), kind=kOutput, calls=%fused_computation.139 | convolution fusion | flops 1623195648 | bytes 9961472 | tf_op jit(solution)/shard_map/ksaf,sbf->kab/dot_general | solution.py:57
  126.6 72.8 %all-reduce.3.cloned.1.call-done = f32[8,64,256]{2,1,0:T(8,128)} async-done(((f32[8,64,256]{2,1,0:T(8,128)}), f32[8,64,256]{2,1,0:T(8,128)}) %all-reduce.3.cloned.1.call-update) | async-done | bytes 524304 | tf_op jit(solution)/shard_map/psum | solution.py:60
  199.5 23.3 %all-gather.5.cloned.1.call-done = f32[8,256,256]{2,1,0:T(8,128)} async-done(((f32[8,64,256]{2,1,0:T(8,128)}), f32[8,256,256]{2,1,0:T(8,128)}) %all-gather.5.cloned.1.call-update) | async-done | bytes 2097168 | tf_op jit(solution)/shard_map/all_gather | solution.py:62
  236.0 4.9 maximum_maximum_fusion
  240.9 5.4 copy.20
  246.2 5.4 fusion.4
  253.6 11.7 %cholesky.223 = f32[128,128]{1,0:T(8,128)S(1)} custom-call(f32[128,128]{1,0:T(8,128)S(1)} %cholesky.580), custom_call_target="Cholesky" | custom-call | tf_op jit(solution)/shard_map/jit(cholesky)/cholesky | solution.py:87
  267.9 9.8 %custom-call.66 = f32[1,128,128]{1,2,0:T(8,128)S(1)} custom-call(f32[1,128,128]{2,1,0:T(8,128)S(1)} %get-tuple-element.63), custom_call_target="InvertDiagBlocksLowerTriangular" | custom-call | tf_op jit(solution)/shard_map/jit(cholesky)/cholesky | solution.py:87
  281.5 11.7 %cholesky.244 = f32[128,128]{1,0:T(8,128)S(1)} custom-call(f32[128,128]{1,0:T(8,128)S(1)} %cholesky.584), custom_call_target="Cholesky" | custom-call | tf_op jit(solution)/shard_map/jit(cholesky)/cholesky | solution.py:87
  295.3 10.0 %custom-call.67 = f32[1,128,128]{1,2,0:T(8,128)S(1)} custom-call(f32[1,128,128]{2,1,0:T(8,128)S(1)} %get-tuple-element.60), custom_call_target="InvertDiagBlocksLowerTriangular" | custom-call | tf_op jit(solution)/shard_map/jit(cholesky)/cholesky | solution.py:87
  308.6 11.7 %cholesky.468 = f32[128,128]{1,0:T(8,128)S(1)} custom-call(f32[128,128]{1,0:T(8,128)S(1)} %cholesky.589), custom_call_target="Cholesky" | custom-call | tf_op jit(solution)/shard_map/jit(cholesky)/cholesky | solution.py:87
  321.7 9.8 %custom-call.68 = f32[1,128,128]{1,2,0:T(8,128)S(1)} custom-call(f32[1,128,128]{2,1,0:T(8,128)S(1)} %get-tuple-element.57), custom_call_target="InvertDiagBlocksLowerTriangular" | custom-call | tf_op jit(solution)/shard_map/jit(cholesky)/cholesky | solution.py:87
  335.1 12.1 %cholesky.487 = f32[128,128]{1,0:T(8,128)S(1)} custom-call(f32[128,128]{1,0:T(8,128)S(1)} %cholesky.594), custom_call_target="Cholesky" | custom-call | tf_op jit(solution)/shard_map/jit(cholesky)/cholesky | solution.py:87
  348.5 9.8 %custom-call.69 = f32[1,128,128]{1,2,0:T(8,128)S(1)} custom-call(f32[1,128,128]{2,1,0:T(8,128)S(1)} %get-tuple-element.54), custom_call_target="InvertDiagBlocksLowerTriangular" | custom-call | tf_op jit(solution)/shard_map/jit(cholesky)/cholesky | solution.py:87
  361.7 11.7 %cholesky.506 = f32[128,128]{1,0:T(8,128)S(1)} custom-call(f32[128,128]{1,0:T(8,128)S(1)} %cholesky.599), custom_call_target="Cholesky" | custom-call | tf_op jit(solution)/shard_map/jit(cholesky)/cholesky | solution.py:87
  374.7 9.8 %custom-call.70 = f32[1,128,128]{1,2,0:T(8,128)S(1)} custom-call(f32[1,128,128]{2,1,0:T(8,128)S(1)} %get-tuple-element.51), custom_call_target="InvertDiagBlocksLowerTriangular" | custom-call | tf_op jit(solution)/shard_map/jit(cholesky)/cholesky | solution.py:87
  388.0 11.7 %cholesky.526 = f32[128,128]{1,0:T(8,128)S(1)} custom-call(f32[128,128]{1,0:T(8,128)S(1)} %cholesky.604), custom_call_target="Cholesky" | custom-call | tf_op jit(solution)/shard_map/jit(cholesky)/cholesky | solution.py:87
  401.0 9.8 %custom-call.71 = f32[1,128,128]{1,2,0:T(8,128)S(1)} custom-call(f32[1,128,128]{2,1,0:T(8,128)S(1)} %get-tuple-element.48), custom_call_target="InvertDiagBlocksLowerTriangular" | custom-call | tf_op jit(solution)/shard_map/jit(cholesky)/cholesky | solution.py:87
  413.9 11.7 %cholesky.546 = f32[128,128]{1,0:T(8,128)S(1)} custom-call(f32[128,128]{1,0:T(8,128)S(1)} %cholesky.609), custom_call_target="Cholesky" | custom-call | tf_op jit(solution)/shard_map/jit(cholesky)/cholesky | solution.py:87
  426.9 10.0 %custom-call.72 = f32[1,128,128]{1,2,0:T(8,128)S(1)} custom-call(f32[1,128,128]{2,1,0:T(8,128)S(1)} %get-tuple-element.45), custom_call_target="InvertDiagBlocksLowerTriangular" | custom-call | tf_op jit(solution)/shard_map/jit(cholesky)/cholesky | solution.py:87
  439.6 11.7 %cholesky.564 = f32[128,128]{1,0:T(8,128)S(1)} custom-call(f32[128,128]{1,0:T(8,128)S(1)} %convolution_subtract_fusion.10), custom_call_target="Cholesky" | custom-call | tf_op jit(solution)/shard_map/jit(cholesky)/cholesky | solution.py:87
  457.7 4.9 select_select_fusion
  462.7 28.7 %while.1 = (s32[]{:T(128)}, f32[1024,1024]{1,0:T(8,128)}, s32[8,2]{0,1:T(2,128)S(1)}, f32[8,128,128]{2,1,0:T(8,128)}, s32[]{:T(128)}) while((s32[]{:T(128)}, f32[1024,1024]{1,0:T(8,128)}, s32[8,2]{0,1:T(2,128)S(1)}, f32[8,128,128]{2,1,0:T(8,128)}, s32[]{:T(128)}) %tuple.96), condition=%wide.while_cond, body=%wide.while_body.sunk | while | flops 2 | bytes 132705 | solution.py:88
  463.3 2.9 bitcast_dynamic-update-slice_fusion.2
  477.7 2.9 bitcast_dynamic-update-slice_fusion.2
  481.3 2.9 bitcast_dynamic-update-slice_fusion.2
  484.9 2.9 bitcast_dynamic-update-slice_fusion.2
  491.3 79.8 %custom-call.73 = f32[8,128,128]{1,2,0:T(8,128)S(1)} custom-call(f32[8,128,128]{2,1,0:T(8,128)} %get-tuple-element.12), custom_call_target="InvertDiagBlocksLowerTriangular" | custom-call | tf_op jit(solution)/shard_map/jit(_cho_solve)/triangular_solve | solution.py:88
  (234 shorter events, 114.1 us)
Async XLA Ops:
  6.5 113.7 %all-gather.3.cloned.1.call-start = ((), (), s32[]{:S(2)}) async-start(), calls=%async_computation | async-start | bytes 3932160 | tf_op jit(solution)/shard_map/all_gather | solution.py:49
  78.7 1.4 copy-start.26
  78.7 2.4 copy-start.28
  78.8 2.4 copy-start.30
  78.8 2.5 copy-start.20
  78.8 2.7 copy-start.22
  78.8 3.7 copy-start.16
  78.8 3.7 copy-start.18
  78.8 4.7 copy-start.12
  78.8 4.7 copy-start.14
  78.8 5.6 copy-start.8
  78.8 5.6 copy-start.10
  78.8 6.6 %copy-start.4 = (bf16[1024,512]{1,0:T(8,128)(2,1)}, bf16[1024,512]{1,0:T(8,128)(2,1)S(1)}, u32[]{:S(2)}) copy-start(bf16[1024,512]{1,0:T(8,128)(2,1)S(1)} %get-tuple-element.108) | copy-start | bytes 3145732
  78.9 6.6 %copy-start.6 = (bf16[1024,512]{1,0:T(8,128)(2,1)}, bf16[1024,512]{1,0:T(8,128)(2,1)S(1)}, u32[]{:S(2)}) copy-start(bf16[1024,512]{1,0:T(8,128)(2,1)S(1)} %get-tuple-element.109) | copy-start | bytes 3145732
  88.8 110.6 %all-reduce.3.cloned.1.call-start = ((), (), s32[]{:S(2)}) async-start(), calls=%async_computation.1 | async-start | bytes 1048576 | tf_op jit(solution)/shard_map/psum | solution.py:60
  126.6 96.2 %all-gather.5.cloned.1.call-start = ((), (), s32[]{:S(2)}) async-start(), calls=%async_computation.2 | async-start | bytes 2621440 | tf_op jit(solution)/shard_map/all_gather | solution.py:62
  251.6 1.9 copy-start.2
  457.7 116.2 %copy-start.34 = (f32[1,256,256]{2,1,0:T(8,128)S(1)}, f32[1,256,256]{2,1,0:T(8,128)}, u32[]{:S(2)}) copy-start(f32[1,256,256]{2,1,0:T(8,128)} %get-tuple-element.32) | copy-start | bytes 786436
  457.7 119.2 %copy-start.33 = (f32[1,256,256]{2,1,0:T(8,128)S(1)}, f32[1,256,256]{2,1,0:T(8,128)}, u32[]{:S(2)}) copy-start(f32[1,256,256]{2,1,0:T(8,128)} %get-tuple-element.31) | copy-start | bytes 786436
  462.7 117.7 %copy-start.32 = (f32[1,256,256]{2,1,0:T(8,128)S(1)}, f32[1,256,256]{2,1,0:T(8,128)}, u32[]{:S(2)}) copy-start(f32[1,256,256]{2,1,0:T(8,128)} %get-tuple-element.27) | copy-start | bytes 786436
  571.1 10.9 %copy-start = (f32[1024,1024]{1,0:T(8,128)S(1)}, f32[1024,1024]{1,0:T(8,128)}, u32[]{:S(2)}) copy-start(f32[1024,1024]{1,0:T(8,128)} %get-tuple-element.184) | copy-start | bytes 12582916
  578.5 8.9 %copy-start.3 = (bf16[6,256,1024]{2,1,0:T(8,128)(2,1)S(1)}, bf16[6,256,1024]{2,1,0:T(8,128)(2,1)}, u32[]{:S(2)}) copy-start(bf16[6,256,1024]{2,1,0:T(8,128)(2,1)} %all-gather.3.cloned.1.call-done) | copy-start | bytes 9437188
  589.9 1.5 copy-start.29
  590.0 1.8 copy-start.31
  591.3 1.4 copy-start.25
  591.4 1.6 copy-start.27
  593.0 1.5 copy-start.23
  594.5 1.5 copy-start.19
  596.1 1.5 copy-start.15
  597.6 1.5 copy-start.11
  599.1 1.5 copy-start.7
  601.7 2.7 copy-start.35
  (7 other events, 8.4 us)
Sparse Core Ops, SparseCore 0:
  88.9 31.2 all-gather.2
  126.7 72.6 all-reduce.2
  201.0 21.7 all-gather.4
where the time goes:
time: 621 us; the launch traced here: 613 us
  other arithmetic  352 us (57%)
  waiting for transfers between devices  121 us (19%)
  matrix products  65 us (10%)
  local copies, waits for them, and re-layouts  54.5 us (9%)
  between operations  20.8 us (3%)
    another operation x31, other arithmetic, shards(): lower_factor = jnp.linalg.cholesky(system)  173 us
    another operation x4, other arithmetic, shards(): filter_own = jax.scipy.linalg.cho_solve((lower_factor, True), rhs)  84.8 us
    psum x1, waiting for transfers between devices, shards(): summed = lax.psum(partial_value, 'shot')  72.8 us
    another operation x2, other arithmetic  72.7 us
    another operation x24, local copies, waits for them, and re-layouts  28.6 us
    all_gather x1, waiting for transfers between devices, shards(): all_spec = lax.all_gather(own_spec, 'lag', axis=1, tiled=True)  24.5 us
    all_gather x1, waiting for transfers between devices, shards(): gathered = lax.all_gather(summed, 'lag', axis=1, tiled=True)  23.3 us
    another operation x14, matrix products, shards(): lower_factor = jnp.linalg.cholesky(system)  23.3 us
  transfers between devices with their start and end apart: 3, of which 3 were waited for; matrix products, arithmetic and copies ran while one was open for 1% of the time, Pallas kernels for 0%

commit v1 on v0

v1 whole, which is shorter than its diff:
```python
import functools

import jax
import jax.numpy as jnp
from jax import lax
from jax.experimental import pallas as pl
from jax.experimental.pallas import tpu as pltpu
from jax.sharding import PartitionSpec as P

LAGS=4
HALF=128
PIVOTS=4

def mm(a, b, dims=((1,), (0,))):
    return lax.dot_general(a, b, (dims, ((), ())), precision=lax.Precision.HIGHEST, preferred_element_type=jnp.float32)


def factor_half(mat):
    lane = lax.broadcasted_iota(jnp.int32, (8, HALF), 1)
    row = lax.broadcasted_iota(jnp.int32, (8, HALF), 0)
    count = HALF // 8
    tiles = [mat[8 * t : 8 * t + 8, :] for t in range(count)]

    def spread(x):
        return jnp.broadcast_to(x, (8, HALF))

    def reduce_by(p, inv, x):
        done = []
        for j in range(PIVOTS):
            value = x[j]
            for i in range(j):
                value = value - p[i, j] * done[i]
            done.append(value * inv[j])
        return done

    for k in range(0, HALF, PIVOTS):
        home, off = k // 8, k % 8
        rows = [spread(tiles[home][off + i : off + i + 1, :]) for i in range(PIVOTS)]
        p = {(i, j): spread(rows[i][:, k + j : k + j + 1]) for i in range(PIVOTS) for j in range(i, PIVOTS)}
        inside = (lane >= k) & (lane < k + PIVOTS)
        rows = [jnp.where(inside, jnp.where(lane == k + i, 1.0, 0.0), rows[i]) for i in range(PIVOTS)]
        inv = []
        for i in range(PIVOTS):
            for m in range(i):
                for j in range(i, PIVOTS):
                    if m == i - 1:
                        p[i, j] = p[i, j] - p[m, i] * p[m, j]
            inv.append(lax.rsqrt(p[i, i]))
            for j in range(i + 1, PIVOTS):
                p[i, j] = p[i, j] * inv[i]
            for l in range(i + 2, PIVOTS):
                for j in range(l, PIVOTS):
                    p[l, j] = p[l, j] - p[i, l] * p[i, j]
        w = reduce_by(p, inv, rows)
        for t in range(home, count):
            if t == home and off + PIVOTS == 8:
                updated = tiles[t]
            else:
                c = reduce_by(p, inv, [spread(tiles[t][:, k + j : k + j + 1]) for j in range(PIVOTS)])
                kept = jnp.where(inside, 0.0, tiles[t])
                updated = kept - ((c[0] * w[0] + c[1] * w[1]) + (c[2] * w[2] + c[3] * w[3]))
            if t == home:
                updated = jnp.where(row < off, tiles[t], updated)
                for i in range(PIVOTS):
                    updated = jnp.where(row == off + i, w[i], updated)
            tiles[t] = updated
    return jnp.concatenate(
        [jnp.where(lane <= row + 8 * t, tiles[t], 0.0) for t in range(count)], axis=0
    )


def solve_kernel(scales, corr_ref, rhs_ref, out_ref, aug, diag, first_inv, coupling):
    channels = corr_ref.shape[1]
    order = LAGS * channels
    width = aug.shape[1]
    block = 2 * HALF
    count = order // block
    local = rhs_ref.shape[-1]

    def scaled(x):
        return x * scales[0] * scales[1]

    for lag in range(LAGS):
        value = scaled(corr_ref[lag])
        if lag == 0:
            same = lax.broadcasted_iota(jnp.int32, value.shape, 0) == lax.broadcasted_iota(jnp.int32, value.shape, 1)
            trace = jnp.sum(jnp.where(same, value, 0.0))
            value = value + jnp.where(same, 0.1 * (trace / channels) + 1e-06, 0.0)
        else:
            flipped = value.T
        for low in range(LAGS - lag):
            high = low + lag
            rows, cols = low * channels, high * channels
            aug[rows : rows + channels, cols : cols + channels] = value if lag == 0 else flipped
    aug[:, order:] = jnp.zeros((order, width - order), jnp.float32)
    for tap in range(LAGS):
        aug[tap * channels : (tap + 1) * channels, order : order + local] = scaled(rhs_ref[tap])
    diag[...] = aug[:HALF, :HALF]

    def step(half_step, carry):
        diag[...] = factor_half(diag[...])
        for b in range(count):
            o = b * block
            mid, end = o + HALF, o + block

            @pl.when(half_step == 2 * b)
            def _():
                low = mm(aug[mid:end, o:mid], diag[...], ((1,), (1,)))
                first_inv[...] = diag[...]
                coupling[...] = low
                diag[...] = aug[mid:end, mid:end] - mm(low, low, ((1,), (1,)))

            @pl.when(half_step == 2 * b + 1)
            def _():
                top, last = first_inv[...], diag[...]
                corner = -mm(last, mm(coupling[...], top))
                aug[o:mid, o:mid] = top
                aug[o:mid, mid:end] = jnp.zeros((HALF, HALF), jnp.float32)
                aug[mid:end, o:mid] = corner
                aug[mid:end, mid:end] = last
                for c in range(end, width, block):
                    ce = min(c + block, width)
                    aug[o:end, c:ce] = mm(aug[o:end, o:end], aug[o:end, c:ce])
                for r in range(end, order, block):
                    left = aug[o:end, r : r + block]
                    for c in range(r, width, block):
                        ce = min(c + block, width)
                        aug[r : r + block, c:ce] = aug[r : r + block, c:ce] - mm(left, aug[o:end, c:ce], ((0,), (0,)))
                if end < order:
                    diag[...] = aug[end : end + HALF, end : end + HALF]

        return carry

    lax.fori_loop(0, 2 * count, step, 0)
    for b in range(count - 1, -1, -1):
        o, end = b * block, (b + 1) * block
        known = aug[o:end, order:]
        if end < order:
            known = known - mm(aug[o:end, end:order], aug[end:order, order:])
        aug[o:end, order:] = mm(aug[o:end, o:end], known, ((0,), (0,)))
    out_ref[...] = aug[:, order : order + local].astype(jnp.bfloat16)


def solve(corr, rhs, scales):
    channels = corr.shape[1]
    local = rhs.shape[-1]
    order = LAGS * channels
    width = order + HALF * pl.cdiv(local, HALF)
    vm = pl.BlockSpec(memory_space=pltpu.VMEM)
    return pl.pallas_call(
        functools.partial(solve_kernel, scales),
        out_shape=jax.ShapeDtypeStruct((order, local), jnp.bfloat16),
        in_specs=[vm, vm],
        out_specs=vm,
        scratch_shapes=[
            pltpu.VMEM((order, width), jnp.float32),
            pltpu.VMEM((HALF, HALF), jnp.float32),
            pltpu.VMEM((HALF, HALF), jnp.float32),
            pltpu.VMEM((HALF, HALF), jnp.float32),
        ],
        compiler_params=pltpu.CompilerParams(vmem_limit_bytes=40 << 20),
        name="block_solve",
    )(corr, rhs)


def dft_table(samples, band_size):
    fine_count = 1
    while fine_count * fine_count < samples:
        fine_count *= 2
    harmonic = jnp.arange(1, band_size + 1, dtype=jnp.int32)

    def circle(times):
        phase = times[:, None] * harmonic[None, :] % (2 * samples)
        angle = phase.astype(jnp.float32) * (jnp.pi / samples)
        return jnp.cos(angle), jnp.sin(angle)

    fine_cos, fine_sin = circle(jnp.arange(fine_count, dtype=jnp.int32))
    coarse_cos, coarse_sin = circle(jnp.arange(samples // fine_count, dtype=jnp.int32) * fine_count)
    first = jnp.concatenate([coarse_cos, coarse_sin], axis=1)[:, None, :]
    second = jnp.concatenate([-coarse_sin, coarse_cos], axis=1)[:, None, :]
    cosines = jnp.concatenate([fine_cos, fine_cos], axis=1)[None]
    sines = jnp.concatenate([fine_sin, fine_sin], axis=1)[None]
    table = (first * cosines + second * sines).astype(jnp.bfloat16)
    return table.reshape(samples, 2 * band_size)


def delay_tables(delays, samples, band_size):
    harmonic = jnp.arange(1, band_size + 1, dtype=jnp.int32)
    phase = delays[:, None] * harmonic[None, :] % (2 * samples)
    angle = phase.astype(jnp.float32) * (jnp.pi / samples)
    return (jnp.cos(angle), jnp.sin(angle))


def delay_apply(spectrum, cosine, sine):
    band_size = cosine.shape[-1]
    real_part = spectrum[..., :band_size]
    imag_part = spectrum[..., band_size:]
    return jnp.concatenate(
        [real_part * cosine - imag_part * sine, imag_part * cosine + real_part * sine], axis=-1
    )


def shards(traces, live_mask, gap_samples):
    shot_count, local_chan, samples = traces.shape
    band_size = samples // 16
    shot_shards = lax.axis_size("shot")
    table = lax.optimization_barrier(dft_table(samples, band_size))
    live_float = live_mask.astype(jnp.float32)[:, :, None]
    running = jnp.einsum("sct,tw->scw", traces, table, preferred_element_type=jnp.float32)
    own_spec = (running * live_float).astype(jnp.bfloat16)
    all_spec = lax.all_gather(own_spec, "lag", axis=1, tiled=True)
    spacing = samples // (2 * band_size)
    tap_delays = jnp.arange(LAGS, dtype=jnp.int32) * spacing
    lag_list = jnp.concatenate([tap_delays, gap_samples[0] + tap_delays])
    cosine, sine = delay_tables(lag_list, samples, band_size)
    rotated = delay_apply(
        own_spec.astype(jnp.float32)[None], cosine[:, None, None, :], sine[:, None, None, :]
    ).astype(jnp.bfloat16)
    partial_value = jnp.einsum(
        "ksaf,sbf->kab", rotated, all_spec, preferred_element_type=jnp.float32
    )
    channels = all_spec.shape[1]
    pieces = partial_value.reshape(shot_shards, -1, channels)
    pieces = lax.all_to_all(pieces, "shot", 0, 0, tiled=False)
    reduced = jnp.sum(pieces, axis=0)
    summed = lax.all_gather(reduced, "shot", axis=0, tiled=True)
    summed = summed.reshape(2 * LAGS, local_chan, channels)
    gathered = lax.all_gather(summed, "lag", axis=1, tiled=True)
    first_out = lax.axis_index("lag") * local_chan
    rhs = lax.dynamic_slice(gathered, (LAGS, 0, first_out), (LAGS, channels, local_chan))
    total_shots = shot_count * shot_shards
    filter_own = solve(gathered[:LAGS], rhs, (1.0 / samples, 1.0 / (samples * total_shots)))
    filter_bf = filter_own.reshape(LAGS, channels, local_chan)
    mixed = jnp.einsum("jab,saf->jsbf", filter_bf, all_spec, preferred_element_type=jnp.float32)
    shifted = delay_apply(mixed, cosine[LAGS:, None, None, :], sine[LAGS:, None, None, :])
    predicted = jnp.sum(shifted, axis=0)
    error = (own_spec.astype(jnp.float32) - predicted).astype(jnp.bfloat16)
    restored = jnp.einsum("scw,tw->sct", error, table, preferred_element_type=jnp.float32)
    return (restored * (1.0 / samples) * live_float).astype(jnp.bfloat16)


def solution(mesh):
    placed = (P("shot", "lag", None), P("shot", "lag"), P())
    return jax.shard_map(
        shards, mesh=mesh, in_specs=placed, out_specs=P("shot", "lag", None), check_vma=False
    )
```

time: 621 us -> 242 us (0.39); the launches traced: 613 us -> 242 us
  other arithmetic: 352 us -> 15.9 us
  waiting for transfers between devices: 121 us -> 46.2 us
  Pallas kernels: 0 us -> 63.3 us
  blocking collectives: 0 us -> 54.2 us
  local copies, waits for them, and re-layouts: 54.5 us -> 8.77 us
  matrix products: 65 us -> 39.4 us
  between operations: 20.8 us -> 14.2 us
    another operation x37 -> x1, other arithmetic: 330 us -> 3.46 us  [the longest x31 173 us: shards(): lower_factor = jnp.linalg.cholesky(system)]
    psum x1 -> x0, waiting for transfers between devices: 72.8 us -> none  [shards(): summed = lax.psum(partial_value, 'shot')]
    pallas_call x0 -> x1, Pallas kernels: none -> 63.3 us  [solve(): pl.pallas_call(functools.partial(solve_kernel, scales), out_shape=jax.Sha...]
    another operation x44 -> x0, matrix products: 38.9 us -> none  [the longest x14 23.3 us: shards(): lower_factor = jnp.linalg.cholesky(system)]
    all_gather x0 -> x1, blocking collectives: none -> 33.6 us  [shards(): summed = lax.all_gather(reduced, 'shot', axis=0, tiled=True)]
    another operation x36 -> x0, local copies, waits for them, and re-layouts: 31.3 us -> none
    all_to_all x0 -> x1, blocking collectives: none -> 20.6 us  [shards(): pieces = lax.all_to_all(pieces, 'shot', 0, 0, tiled=False)]
    dot_general x8 -> x1, matrix products: 9.31 us -> 24 us  [shards(): jnp.einsum('scw,tw->sct', error, table, preferred_element_type=jnp.float32)]
  transfers between devices with their start and end apart: 3 -> 2, of which waited for: 3 -> 2; matrix products, arithmetic and copies ran while one was open for 1% -> 2% of each run, Pallas kernels for 0% -> 0%
where the time goes in v1:
time: 242 us
  Pallas kernels  63.3 us (26%)
  blocking collectives  54.2 us (22%)
  waiting for transfers between devices  46.2 us (19%)
  matrix products  39.4 us (16%)
  other arithmetic  15.9 us (7%)
  between operations  14.2 us (6%)
  local copies, waits for them, and re-layouts  8.77 us (4%)
    pallas_call x1, Pallas kernels, solve(): pl.pallas_call(functools.partial(solve_kernel, scales), out_shape=jax.Sha...  63.3 us
    all_gather x1, blocking collectives, shards(): summed = lax.all_gather(reduced, 'shot', axis=0, tiled=True)  33.6 us
    all_gather x1, waiting for transfers between devices, shards(): all_spec = lax.all_gather(own_spec, 'lag', axis=1, tiled=True)  25.6 us
    dot_general x1, matrix products, shards(): jnp.einsum('scw,tw->sct', error, table, preferred_element_type=jnp.float32)  24 us
    all_gather x1, waiting for transfers between devices, shards(): gathered = lax.all_gather(summed, 'lag', axis=1, tiled=True)  20.6 us
    all_to_all x1, blocking collectives, shards(): pieces = lax.all_to_all(pieces, 'shot', 0, 0, tiled=False)  20.6 us
    dot_general x1, matrix products, shards(): jnp.einsum('sct,tw->scw', traces, table, preferred_element_type=jnp.float32)  9.7 us
    unnamed x8, local copies, waits for them, and re-layouts  6.09 us
  transfers between devices with their start and end apart: 2, of which 2 were waited for; matrix products, arithmetic and copies ran while one was open for 2% of the time, Pallas kernels for 0%

profile of v1, /device:TPU:0, one launch (start us, length us, event | category | flops | bytes accessed | tf_op | source)
XLA Modules:
  0.0 242.1 jit_solution(15593232840762467511)
XLA Ops:
  6.5 0.0 all-gather.3.cloned.1.call-start
  6.5 1.0 fusion.38
  7.6 0.6 fusion.39
  8.2 0.1 pad_maximum_fusion
  8.3 0.1 pad_maximum_fusion.2
  8.4 0.0 copy-start.3
  8.4 6.0 %add_convert_fusion = bf16[64,128,1024]{2,1,0:T(8,128)(2,1)S(1)} fusion(f32[128,1024]{1,0:T(8,128)S(1)} %get-tuple-element.21, f32[64,1024]{1,0:T(8,128)S(1)} %get-tuple-element.12, f32[128,1024]{1,0:T(8,128)S(1)} %get-tuple-element.20, f32[64,1024]{1,0:T(8,128)S(1)} %get-tuple-element.11), kind=kLoop, calls=%fused_computation | loop fusion | flops 33554432 | bytes 18350080 | tf_op jit(solution)/shard_map/convert_element_type | solution.py:183
  14.4 0.0 copy-start
  14.5 5.7 %copy-done = bf16[64,128,1024]{2,1,0:T(8,128)(2,1)} copy-done((bf16[64,128,1024]{2,1,0:T(8,128)(2,1)}, bf16[64,128,1024]{2,1,0:T(8,128)(2,1)S(1)}, u32[]{:S(2)}) %copy-start) | copy-done | bytes 16777240
  20.2 9.7 %fusion.19 = bf16[6,64,1024]{2,1,0:T(8,128)(2,1)} fusion(bf16[6,64,8192]{2,1,0:T(8,128)(2,1)} %param.3, bf16[8192,1024]{1,0:T(8,128)(2,1)S(1)} %bitcast.45, f32[6,64]{1,0:T(8,128)S(1)} %convert_element_type.59), kind=kOutput, calls=%fused_computation.23 | convolution fusion | flops 6443237376 | bytes 23856640 | tf_op jit(solution)/shard_map/sct,tw->scw/dot_general | solution.py:209
  29.9 0.0 all-gather.3.cloned.1.call-update
  29.9 0.0 all-gather.5.cloned.1.call-start
  30.6 0.1 pad_add_fusion
  30.7 0.2 fusion.46
  30.8 1.3 convert_bitcast_fusion
  32.1 0.1 slice_bitcast_fusion.1
  32.3 3.5 %subtract_convert_fusion = (bf16[8,6,64,512]{3,2,1,0:T(8,128)(2,1)S(1)}, bf16[8,6,64,512]{3,2,1,0:T(8,128)(2,1)}) fusion(f32[8,512]{1,0:T(8,128)S(1)} %get-tuple-element.14, f32[6,64,512]{2,1,0:T(8,128)S(1)} %get-tuple-element.10, f32[8,512]{1,0:T(8,128)S(1)} %get-tuple-element.13, f32[6,64,512]{2,1,0:T(8,128)S(1)} %get-tuple-element.9), kind=kLoop, calls=%fused_computation.12 | loop fusion | flops 12582912 | bytes 7897088 | tf_op jit(solution)/shard_map/convert
  35.7 25.6 %all-gather.3.cloned.1.call-done = bf16[6,256,1024]{2,1,0:T(8,128)(2,1)} async-done(((bf16[6,64,1024]{2,1,0:T(8,128)(2,1)}), bf16[6,256,1024]{2,1,0:T(8,128)(2,1)}) %all-gather.3.cloned.1.call-update) | async-done | bytes 3145744 | tf_op jit(solution)/shard_map/all_gather | solution.py:211
  61.3 4.4 %fusion.22 = f32[8,64,256]{2,1,0:T(8,128)S(1)} fusion(bf16[6,256,1024]{2,1,0:T(8,128)(2,1)} %all-gather.3.cloned.1.call-done, bf16[8,6,64,512]{3,2,1,0:T(8,128)(2,1)} %get-tuple-element.8, bf16[8,6,64,512]{3,2,1,0:T(8,128)(2,1)S(1)} %get-tuple-element.7), kind=kOutput, calls=%fused_computation.24 | convolution fusion | flops 1623195648 | bytes 9961472 | tf_op jit(solution)/shard_map/ksaf,sbf->kab/dot_general | solution.py:219
  65.8 20.6 %all_to_all.5 = f32[8,64,256]{2,1,0:T(8,128)} all-to-all(f32[8,64,256]{2,1,0:T(8,128)S(1)} %fusion.22), channel_id=1, replica_groups=mesh['shot'=8,'lag'=4] {'shot'}, dimensions={0} | all-to-all | bytes 1048576 | tf_op jit(solution)/shard_map/all_to_all | solution.py:224
  86.3 1.1 reduce_sum.18
  87.4 33.6 %all_gather.10 = f32[512,256]{1,0:T(8,128)} all-gather(f32[64,256]{1,0:T(8,128)S(1)} %reduce_sum.18), channel_id=1, replica_groups=mesh['shot'=8,'lag'=4] {'shot'}, dimensions={0}, use_global_device_ids=true | all-gather | bytes 589824 | tf_op jit(solution)/shard_map/all_gather | solution.py:226
  121.0 0.0 all-gather.5.cloned.1.call-update
  121.1 20.6 %all-gather.5.cloned.1.call-done = f32[8,256,256]{2,1,0:T(8,128)} async-done(((f32[8,64,256]{2,1,0:T(8,128)}), f32[8,256,256]{2,1,0:T(8,128)}) %all-gather.5.cloned.1.call-update) | async-done | bytes 2097168 | tf_op jit(solution)/shard_map/all_gather | solution.py:228
  141.7 1.3 slice.30.corr_ref
  143.0 1.2 constant_dynamic-slice_fusion.rhs_ref
  144.3 63.3 %block_solve.1 = bf16[1024,64]{1,0:T(8,128)(2,1)S(1)} custom-call(f32[4,256,256]{2,1,0:T(8,128)S(1)} %slice.30.corr_ref, f32[4,256,64]{2,1,0:T(8,128)S(1)} %constant_dynamic-slice_fusion.rhs_ref), custom_call_target="tpu_custom_call" | custom-call | tf_op jit(solution)/shard_map/block_solve/pallas_call | solution.py:150
  207.6 1.2 fusion.13
  208.8 1.2 multiply_subtract_fusion
  210.0 0.7 maximum_reduce_fusion
  210.8 0.4 copy-done.1
  211.2 24.0 %multiply_convert_fusion = bf16[6,64,8192]{2,1,0:T(8,128)(2,1)} fusion(bf16[8192,1024]{1,0:T(8,128)(2,1)} %bitcast.46, f32[6,64]{1,0:T(8,128)S(1)} %broadcast_multiply_fusion, f32[6,64,1024]{2,1,0:T(8,128)S(1)} %maximum_reduce_fusion, bf16[6,64,1024]{2,1,0:T(8,128)(2,1)S(1)} %copy-done.1), kind=kOutput, calls=%fused_computation.5 | convolution fusion | flops 6449922048 | bytes 25429504 | tf_op jit(solution)/shard_map/scw,tw->sct/dot_general | solution.py:238
  (11 shorter events, 0.0 us)
Async XLA Ops:
  6.5 54.8 %all-gather.3.cloned.1.call-start = ((), (), s32[]{:S(2)}) async-start(), calls=%async_computation.1 | async-start | bytes 3932160 | tf_op jit(solution)/shard_map/all_gather | solution.py:211
  8.4 6.1 %copy-start.3 = (s32[6,64]{1,0:T(8,128)S(1)}, s32[6,64]{1,0:T(8,128)}, u32[]{:S(2)}) copy-start(s32[6,64]{1,0:T(8,128)} %param.4) | copy-start | bytes 4612
  14.4 5.7 %copy-start = (bf16[64,128,1024]{2,1,0:T(8,128)(2,1)}, bf16[64,128,1024]{2,1,0:T(8,128)(2,1)S(1)}, u32[]{:S(2)}) copy-start(bf16[64,128,1024]{2,1,0:T(8,128)(2,1)S(1)} %add_convert_fusion) | copy-start | bytes 50331652
  29.9 111.8 %all-gather.5.cloned.1.call-start = ((), (), s32[]{:S(2)}) async-start(), calls=%async_computation.2 | async-start | bytes 2621440 | tf_op jit(solution)/shard_map/all_gather | solution.py:228
  65.7 141.8 %copy-start.2 = (bf16[6,256,1024]{2,1,0:T(8,128)(2,1)S(1)}, bf16[6,256,1024]{2,1,0:T(8,128)(2,1)}, u32[]{:S(2)}) copy-start(bf16[6,256,1024]{2,1,0:T(8,128)(2,1)} %all-gather.3.cloned.1.call-done) | copy-start | bytes 9437188
  210.0 1.1 copy-start.1
Sparse Core Ops, SparseCore 0:
  30.0 31.2 all-gather.2
  121.2 20.4 all-gather.4

commit v2 on v1

--- a/solution.py
+++ b/solution.py
@@ -184,6 +184,32 @@
     return table.reshape(samples, 2 * band_size)
 
 
+def restore_kernel(scale, error_ref, table_ref, live_ref, out_ref):
+    value = lax.dot_general(
+        error_ref[...], table_ref[...], (((1,), (1,)), ((), ())), preferred_element_type=jnp.float32
+    )
+    out_ref[...] = (value * scale * live_ref[...]).astype(jnp.bfloat16)
+
+
+def restore(error, table, live):
+    rows, depth = error.shape
+    samples = table.shape[0]
+    step = min(1024, samples)
+    return pl.pallas_call(
+        functools.partial(restore_kernel, 1.0 / samples),
+        out_shape=jax.ShapeDtypeStruct((rows, samples), jnp.bfloat16),
+        grid=(samples // step,),
+        in_specs=[
+            pl.BlockSpec((rows, depth), lambda t: (0, 0)),
+            pl.BlockSpec((step, depth), lambda t: (t, 0)),
+            pl.BlockSpec((rows, 1), lambda t: (0, 0)),
+        ],
+        out_specs=pl.BlockSpec((rows, step), lambda t: (0, t)),
+        compiler_params=pltpu.CompilerParams(vmem_limit_bytes=24 << 20),
+        name="restore",
+    )(error, table, live)
+
+
 def delay_tables(delays, samples, band_size):
     harmonic = jnp.arange(1, band_size + 1, dtype=jnp.int32)
     phase = delays[:, None] * harmonic[None, :] % (2 * samples)
@@ -223,7 +249,8 @@
     pieces = partial_value.reshape(shot_shards, -1, channels)
     pieces = lax.all_to_all(pieces, "shot", 0, 0, tiled=False)
     reduced = jnp.sum(pieces, axis=0)
-    summed = lax.all_gather(reduced, "shot", axis=0, tiled=True)
+    copies = jnp.broadcast_to(reduced[None], (shot_shards,) + reduced.shape)
+    summed = lax.all_to_all(copies, "shot", 0, 0, tiled=False)
     summed = summed.reshape(2 * LAGS, local_chan, channels)
     gathered = lax.all_gather(summed, "lag", axis=1, tiled=True)
     first_out = lax.axis_index("lag") * local_chan
@@ -235,8 +262,9 @@
     shifted = delay_apply(mixed, cosine[LAGS:, None, None, :], sine[LAGS:, None, None, :])
     predicted = jnp.sum(shifted, axis=0)
     error = (own_spec.astype(jnp.float32) - predicted).astype(jnp.bfloat16)
-    restored = jnp.einsum("scw,tw->sct", error, table, preferred_element_type=jnp.float32)
-    return (restored * (1.0 / samples) * live_float).astype(jnp.bfloat16)
+    rows = shot_count * local_chan
+    restored = restore(error.reshape(rows, -1), table, live_float.reshape(rows, 1))
+    return restored.reshape(shot_count, local_chan, samples)
 
 
 def solution(mesh):

time: 242 us -> 214 us (0.88)
  matrix products: 39.4 us -> 15.4 us
  blocking collectives: 54.2 us -> 38.5 us
  Pallas kernels: 63.3 us -> 72.4 us
  local copies, waits for them, and re-layouts: 8.77 us -> 11.7 us
    all_gather x1 -> x0, blocking collectives: 33.6 us -> none  [shards(): summed = lax.all_gather(reduced, 'shot', axis=0, tiled=True)]
    dot_general x1 -> x0, matrix products: 24 us -> none  [shards(): jnp.einsum('scw,tw->sct', error, table, preferred_element_type=jnp.float32)]
    all_to_all x0 -> x1, blocking collectives: none -> 18.3 us  [shards(): summed = lax.all_to_all(copies, 'shot', 0, 0, tiled=False)]
    pallas_call x0 -> x1, Pallas kernels: none -> 9.07 us  [restore(): pl.pallas_call(functools.partial(restore_kernel, 1.0 / samples), out_shap...]
    unnamed x8 -> x16, local copies, waits for them, and re-layouts: 6.09 us -> 8.8 us
where the time goes in v2:
time: 214 us; the launch traced here: 213 us
  Pallas kernels  72.4 us (34%)
  waiting for transfers between devices  46.2 us (22%)
  blocking collectives  38.5 us (18%)
  matrix products  15.4 us (7%)
  other arithmetic  14.8 us (7%)
  between operations  14.3 us (7%)
  local copies, waits for them, and re-layouts  11.7 us (5%)
    pallas_call x1, Pallas kernels, solve(): pl.pallas_call(functools.partial(solve_kernel, scales), out_shape=jax.Sha...  63.3 us
    all_gather x1, waiting for transfers between devices, shards(): all_spec = lax.all_gather(own_spec, 'lag', axis=1, tiled=True)  25.6 us
    all_gather x1, waiting for transfers between devices, shards(): gathered = lax.all_gather(summed, 'lag', axis=1, tiled=True)  20.6 us
    all_to_all x1, blocking collectives, shards(): pieces = lax.all_to_all(pieces, 'shot', 0, 0, tiled=False)  20.2 us
    all_to_all x1, blocking collectives, shards(): summed = lax.all_to_all(copies, 'shot', 0, 0, tiled=False)  18.3 us
    dot_general x1, matrix products, shards(): jnp.einsum('sct,tw->scw', traces, table, preferred_element_type=jnp.float32)  9.7 us
    pallas_call x1, Pallas kernels, restore(): pl.pallas_call(functools.partial(restore_kernel, 1.0 / samples), out_shap...  9.07 us
    unnamed x16, local copies, waits for them, and re-layouts  8.8 us
  transfers between devices with their start and end apart: 2, of which 2 were waited for; matrix products, arithmetic and copies ran while one was open for 2% of the time, Pallas kernels for 0%

profile of v2, /device:TPU:0, one launch (start us, length us, event | category | flops | bytes accessed | tf_op | source)
XLA Modules:
  0.0 213.3 jit_solution(17360234142216722580)
XLA Ops:
  6.5 1.0 fusion.33
  7.6 0.6 fusion.34
  8.2 0.1 pad_maximum_fusion
  8.3 0.1 pad_maximum_fusion.2
  8.4 6.0 %add_convert_fusion = bf16[64,128,1024]{2,1,0:T(8,128)(2,1)S(1)} fusion(f32[128,1024]{1,0:T(8,128)S(1)} %get-tuple-element.21, f32[64,1024]{1,0:T(8,128)S(1)} %get-tuple-element.12, f32[128,1024]{1,0:T(8,128)S(1)} %get-tuple-element.20, f32[64,1024]{1,0:T(8,128)S(1)} %get-tuple-element.11), kind=kLoop, calls=%fused_computation | loop fusion | flops 33554432 | bytes 18350080 | tf_op jit(solution)/shard_map/convert_element_type | solution.py:183
  14.5 9.7 %fusion.15 = bf16[6,64,1024]{2,1,0:T(8,128)(2,1)} fusion(bf16[6,64,8192]{2,1,0:T(8,128)(2,1)} %param.3, bf16[8192,1024]{1,0:T(8,128)(2,1)S(1)} %bitcast.41, f32[6,64]{1,0:T(8,128)S(1)} %convert_element_type.56), kind=kOutput, calls=%fused_computation.20 | convolution fusion | flops 6443237376 | bytes 23856640 | tf_op jit(solution)/shard_map/sct,tw->scw/dot_general | solution.py:235
  24.2 5.7 %copy-done = bf16[64,128,1024]{2,1,0:T(8,128)(2,1)} copy-done((bf16[64,128,1024]{2,1,0:T(8,128)(2,1)}, bf16[64,128,1024]{2,1,0:T(8,128)(2,1)S(1)}, u32[]{:S(2)}) %copy-start) | copy-done | bytes 16777240
  29.9 0.0 all-gather.3.cloned.1.call-update
  29.9 0.0 all-gather.5.cloned.1.call-start
  30.6 0.1 pad_add_fusion
  30.7 0.2 fusion.41
  30.8 1.3 convert_bitcast_fusion
  32.2 0.1 slice_bitcast_fusion.1
  32.3 3.5 %subtract_convert_fusion = (bf16[8,6,64,512]{3,2,1,0:T(8,128)(2,1)S(1)}, bf16[8,6,64,512]{3,2,1,0:T(8,128)(2,1)}) fusion(f32[8,512]{1,0:T(8,128)S(1)} %get-tuple-element.14, f32[6,64,512]{2,1,0:T(8,128)S(1)} %get-tuple-element.10, f32[8,512]{1,0:T(8,128)S(1)} %get-tuple-element.13, f32[6,64,512]{2,1,0:T(8,128)S(1)} %get-tuple-element.9), kind=kLoop, calls=%fused_computation.9 | loop fusion | flops 12582912 | bytes 7897088 | tf_op jit(solution)/shard_map/convert
  35.7 25.6 %all-gather.3.cloned.1.call-done = bf16[6,256,1024]{2,1,0:T(8,128)(2,1)} async-done(((bf16[6,64,1024]{2,1,0:T(8,128)(2,1)}), bf16[6,256,1024]{2,1,0:T(8,128)(2,1)}) %all-gather.3.cloned.1.call-update) | async-done | bytes 3145744 | tf_op jit(solution)/shard_map/all_gather | solution.py:237
  61.3 4.4 %fusion.18 = f32[8,64,256]{2,1,0:T(8,128)S(1)} fusion(bf16[6,256,1024]{2,1,0:T(8,128)(2,1)} %all-gather.3.cloned.1.call-done, bf16[8,6,64,512]{3,2,1,0:T(8,128)(2,1)} %get-tuple-element.8, bf16[8,6,64,512]{3,2,1,0:T(8,128)(2,1)S(1)} %get-tuple-element.7), kind=kOutput, calls=%fused_computation.21 | convolution fusion | flops 1623195648 | bytes 9961472 | tf_op jit(solution)/shard_map/ksaf,sbf->kab/dot_general | solution.py:245
  65.8 20.2 %all_to_all.10 = f32[8,64,256]{2,1,0:T(8,128)S(1)} all-to-all(f32[8,64,256]{2,1,0:T(8,128)S(1)} %fusion.18), channel_id=1, replica_groups=mesh['shot'=8,'lag'=4] {'shot'}, dimensions={0} | all-to-all | bytes 1048576 | tf_op jit(solution)/shard_map/all_to_all | solution.py:250
  86.1 18.3 %all_to_all.11 = f32[8,64,256]{2,1,0:T(8,128)} all-to-all(f32[8,64,256]{2,1,0:T(8,128)S(1)} %broadcast_in_dim.5), channel_id=1, replica_groups=mesh['shot'=8,'lag'=4] {'shot'}, dimensions={0} | all-to-all | bytes 1048576 | tf_op jit(solution)/shard_map/all_to_all | solution.py:253
  104.3 0.0 all-gather.5.cloned.1.call-update
  104.4 0.2 reshape_broadcast_in_dim.4.live_ref
  104.6 20.6 %all-gather.5.cloned.1.call-done = f32[8,256,256]{2,1,0:T(8,128)} async-done(((f32[8,64,256]{2,1,0:T(8,128)}), f32[8,256,256]{2,1,0:T(8,128)}) %all-gather.5.cloned.1.call-update) | async-done | bytes 2097168 | tf_op jit(solution)/shard_map/all_gather | solution.py:255
  125.2 1.3 slice.30.corr_ref
  126.5 1.2 constant_dynamic-slice_fusion.rhs_ref
  127.7 63.3 %block_solve.1 = bf16[1024,64]{1,0:T(8,128)(2,1)S(1)} custom-call(f32[4,256,256]{2,1,0:T(8,128)S(1)} %slice.30.corr_ref, f32[4,256,64]{2,1,0:T(8,128)S(1)} %constant_dynamic-slice_fusion.rhs_ref), custom_call_target="tpu_custom_call" | custom-call | tf_op jit(solution)/shard_map/block_solve/pallas_call | solution.py:150
  191.1 1.3 fusion.9
  192.4 0.8 multiply_subtract_fusion
  193.2 0.8 maximum_reduce_fusion
  194.0 1.1 copy-done.1
  195.1 0.3 fusion.12
  195.4 0.7 slice-done.2
  196.2 1.2 slice-done.3
  197.4 9.1 %restore.1 = bf16[384,8192]{1,0:T(8,128)(2,1)} custom-call(bf16[384,1024]{1,0:T(8,128)(2,1)S(1)} %bitcast.45, bf16[8192,1024]{1,0:T(8,128)(2,1)S(1)} %bitcast.44, f32[384,1]{1,0:T(8,128)S(1)} %reshape_broadcast_in_dim.4.live_ref), custom_call_target="tpu_custom_call" | custom-call | tf_op jit(solution)/shard_map/restore/pallas_call | solution.py:198
  (22 shorter events, 0.1 us)
Async XLA Ops:
  6.5 54.8 %all-gather.3.cloned.1.call-start = ((), (), s32[]{:S(2)}) async-start(), calls=%async_computation.2 | async-start | bytes 3932160 | tf_op jit(solution)/shard_map/all_gather | solution.py:237
  8.4 6.1 %copy-start.3 = (s32[6,64]{1,0:T(8,128)S(1)}, s32[6,64]{1,0:T(8,128)}, u32[]{:S(2)}) copy-start(s32[6,64]{1,0:T(8,128)} %param.4) | copy-start | bytes 4612
  24.2 5.7 %copy-start = (bf16[64,128,1024]{2,1,0:T(8,128)(2,1)}, bf16[64,128,1024]{2,1,0:T(8,128)(2,1)S(1)}, u32[]{:S(2)}) copy-start(bf16[64,128,1024]{2,1,0:T(8,128)(2,1)S(1)} %add_convert_fusion) | copy-start | bytes 50331652
  29.9 95.3 %all-gather.5.cloned.1.call-start = ((), (), s32[]{:S(2)}) async-start(), calls=%async_computation.3 | async-start | bytes 2621440 | tf_op jit(solution)/shard_map/all_gather | solution.py:255
  86.0 105.0 %copy-start.2 = (bf16[6,256,1024]{2,1,0:T(8,128)(2,1)S(1)}, bf16[6,256,1024]{2,1,0:T(8,128)(2,1)}, u32[]{:S(2)}) copy-start(bf16[6,256,1024]{2,1,0:T(8,128)(2,1)} %all-gather.3.cloned.1.call-done) | copy-start | bytes 9437188
  191.1 4.3 %slice-start = ((s8[16777216]{0:T(1024)(128)(4,1)}), s8[4194304]{0:T(1024)(128)(4,1)S(1)}, s32[]{:S(2)}) async-start(s8[16777216]{0:T(1024)(128)(4,1)} %bitcast.42), calls=%async_computation.4 | async-start | bytes 8388608
  191.1 4.3 %slice-start.1 = ((s8[16777216]{0:T(1024)(128)(4,1)}), s8[4194304]{0:T(1024)(128)(4,1)S(1)}, s32[]{:S(2)}) async-start(s8[16777216]{0:T(1024)(128)(4,1)} %bitcast.42), calls=%async_computation.5 | async-start | bytes 8388608
  192.4 3.8 %slice-start.2 = ((s8[16777216]{0:T(1024)(128)(4,1)}), s8[4194304]{0:T(1024)(128)(4,1)S(1)}, s32[]{:S(2)}) async-start(s8[16777216]{0:T(1024)(128)(4,1)} %bitcast.42), calls=%async_computation.6 | async-start | bytes 8388608
  193.2 1.9 copy-start.1
  193.2 4.1 %slice-start.3 = ((s8[16777216]{0:T(1024)(128)(4,1)}), s8[4194304]{0:T(1024)(128)(4,1)S(1)}, s32[]{:S(2)}) async-start(s8[16777216]{0:T(1024)(128)(4,1)} %bitcast.42), calls=%async_computation.7 | async-start | bytes 8388608
Sparse Core Ops, SparseCore 0:
  30.0 31.2 all-gather.2
  104.5 20.6 all-gather.4
